TPU v7x, 128 devices: a whole 4x4x4 slice. The times are simulated.
128 devices in a mesh: seq: 32 (over z_lo, y, x), fsdp: 4 (over z_hi, core).
Axes of the slice: x: 4, y: 4, z: 4 (z_hi: 2, z_lo: 2; z = z_hi * 2 + z_lo), core: 2. Of those that a mesh axis runs over, the one named last changes fastest.
Arguments:
- tokens: bfloat16 [4, 8192, 2048], P('fsdp', 'seq'), may hold values from -6 to 6
- w_in: bfloat16 [2048, 2304], P('fsdp'), may hold values from -0.125 to 0.125
- log_decay: float32 [4, 32, 8192], P('fsdp', None, 'seq'), may hold values from -2 to 0, as said below
- grad_out: bfloat16 [4, 8192, 2048], P('fsdp', 'seq'), may hold values from -6 to 6
Outputs:
- mixer_out: bfloat16 [4, 8192, 2048], P('fsdp', 'seq')
- grad_tokens: bfloat16 [4, 8192, 2048], P('fsdp', 'seq')
- grad_weights: float32 [2048, 2304], P(('seq', 'fsdp'))
Inputs may be any that keep to these rules, and one draw needn't show every extreme that they name: `log_decay`: each entry is the logarithm of a decay factor below one.
All inputs are finite; a program needn't handle non-finite values.
Results may differ from a plain program's by a relative error of at most 0.015.
Values may be sent and summed in bfloat16 or wider, within the bound.
A program may use at most 192 MiB of HBM per device.

v0:
```python
import jax
import jax.numpy as jnp
from jax import lax
from jax.sharding import PartitionSpec as P

BLOCK = 256
highest = lax.Precision.HIGHEST
epsilon = 1e-05


def entering_2(shard, axis, join, neutral, backward):
    count = lax.axis_size(axis)
    place = lax.axis_index(axis)
    ahead = count - 1 - place if backward else place
    gathered = jax.tree.map(
        lambda a, kind: lax.all_gather(a.astype(kind), axis), shard, (jnp.bfloat16, jnp.bfloat16)
    )
    state = jax.tree.map(lambda a, e: jnp.zeros_like(a) + jnp.asarray(e, a.dtype), shard, neutral)

    def one(step, state):
        source = count - 1 - step if backward else step
        return join(
            state,
            jax.tree.map(
                lambda a, own: lax.dynamic_index_in_dim(a, source, 0, False).astype(own.dtype),
                gathered,
                shard,
            ),
        )

    return lax.fori_loop(0, ahead, one, state)


def combine_states(earlier, latter):
    return (earlier[0] + latter[0], jnp.exp(latter[0])[:, None, None] * earlier[1] + latter[1])


def block_chain(log_rates, terms, backward, start_state):

    def advance(carried, packed):
        log_k, term_k = packed
        return (jnp.exp(log_k)[:, None, None] * carried + term_k, carried)

    finish, inputs = lax.scan(advance, start_state, (log_rates, terms), reverse=backward)
    return (inputs, finish)


def decay_matrix(cumulative, log_rates):
    extent = cumulative.shape[-1]
    row_idx = lax.broadcasted_iota(jnp.int32, (extent, extent), 0)
    col_idx = lax.broadcasted_iota(jnp.int32, (extent, extent), 1)
    later_gap = cumulative[:, :, None] - cumulative[:, None, :]
    exclusive = cumulative - log_rates
    earlier_gap = exclusive[:, None, :] - exclusive[:, :, None]
    exponent = jnp.where(
        row_idx > col_idx, later_gap, jnp.where(row_idx < col_idx, earlier_gap, 0.0)
    )
    return jnp.exp(exponent) + (row_idx == col_idx).astype(jnp.float32)


def to_groups(array, axis, per_group):
    extents = array.shape
    grouped_shape = extents[:axis] + (extents[axis] // per_group, per_group) + extents[axis + 1 :]
    return jnp.moveaxis(array.reshape(grouped_shape), axis, 0)


def from_groups(array, axis):
    moved = jnp.moveaxis(array, 0, axis)
    extents = moved.shape
    return moved.reshape(
        extents[:axis] + (extents[axis] * extents[axis + 1],) + extents[axis + 2 :]
    )


def on_device(tokens, w_in, log_decay, grad_out):
    local_tokens = tokens[0]
    log_rates = log_decay[0]
    upstream_grad = grad_out[0]
    token_count = local_tokens.shape[0]
    hidden_width = local_tokens.shape[1]
    head_count = log_rates.shape[0]
    col_count = w_in.shape[1]
    inner_width = upstream_grad.shape[1]
    head_size = inner_width // head_count
    state_size = (col_count - inner_width) // 2
    block_count = token_count // BLOCK
    per_group = 8
    projected = jnp.dot(
        local_tokens,
        lax.all_gather(w_in, "fsdp", axis=0, tiled=True),
        preferred_element_type=jnp.float32,
    )
    xbc_rows = projected.astype(jnp.bfloat16)
    xbc_rows = lax.optimization_barrier(xbc_rows)
    xbc_float = xbc_rows.astype(jnp.float32)
    values = xbc_float[:, :inner_width].reshape(block_count, BLOCK, head_count, head_size)
    key_rows = xbc_float[:, inner_width : inner_width + state_size].reshape(
        block_count, BLOCK, state_size
    )
    queries = xbc_float[:, inner_width + state_size :].reshape(block_count, BLOCK, state_size)
    key_half = xbc_rows[:, inner_width : inner_width + state_size].reshape(
        block_count, BLOCK, state_size
    )
    query_half = xbc_rows[:, inner_width + state_size :].reshape(block_count, BLOCK, state_size)
    blocked = log_rates.reshape(head_count, block_count, BLOCK).transpose(1, 0, 2)
    cumulative = jnp.cumsum(blocked, axis=-1)
    totals = cumulative[:, :, -1]
    to_end = jnp.exp(totals[:, :, None] - cumulative)
    from_start = jnp.exp(cumulative - blocked)
    enter_weight = jnp.exp(cumulative)
    leave_weight = jnp.exp(totals[:, :, None] - (cumulative - blocked))
    end_terms = jnp.einsum("khq,kqhp,kqn->khpn", to_end, values, key_rows, precision=highest)
    start_terms = jnp.einsum("khq,kqhp,kqn->khpn", from_start, values, key_rows, precision=highest)
    zero_state = jnp.zeros((head_count, head_size, state_size), jnp.float32)
    none_log = jnp.zeros((head_count,), jnp.float32)
    device_log = jnp.sum(totals, axis=0)
    _, end_total = block_chain(totals, end_terms, False, zero_state)
    _, start_total = block_chain(totals, start_terms, True, zero_state)
    entering = entering_2(
        (device_log, end_total), "seq", combine_states, (none_log, zero_state), False
    )[1]
    arriving = entering_2(
        (device_log, start_total), "seq", combine_states, (none_log, zero_state), True
    )[1]
    fwd_in, _ = block_chain(totals, end_terms, False, entering)
    rev_next, _ = block_chain(totals, start_terms, True, arriving)

    def block_forward(packed):
        (
            block_vals,
            block_khalf,
            block_qhalf,
            block_queries,
            block_cumul,
            block_logs,
            block_enter,
            block_leave,
            state_in,
            state_next,
        ) = packed
        affinity = lax.dot_general(
            block_qhalf, block_khalf, (((1,), (1,)), ((), ())), preferred_element_type=jnp.float32
        )

        def group_forward(section):
            group_values, group_cumul, group_logs = section
            weighted = affinity[None] * decay_matrix(group_cumul, group_logs)
            return jnp.einsum("gij,jgp->igp", weighted, group_values, precision=highest)

        group_parts = lax.map(
            group_forward,
            (
                to_groups(block_vals, 1, per_group),
                to_groups(block_cumul, 0, per_group),
                to_groups(block_logs, 0, per_group),
            ),
        )
        inner_part = from_groups(group_parts, 1)
        carried_in = (
            jnp.einsum("qn,hpn->qhp", block_queries, state_in, precision=highest)
            * block_enter.T[:, :, None]
        )
        carried_back = (
            jnp.einsum("qn,hpn->qhp", block_queries, state_next, precision=highest)
            * block_leave.T[:, :, None]
        )
        return inner_part + carried_in + carried_back

    mixture = lax.map(
        block_forward,
        (
            values,
            key_half,
            query_half,
            queries,
            cumulative,
            blocked,
            enter_weight,
            leave_weight,
            fwd_in,
            rev_next,
        ),
    )
    row_scale = jnp.sqrt(jnp.mean(mixture * mixture, axis=-1) + epsilon)
    normed = mixture / row_scale[..., None]
    mixer_out = normed.astype(jnp.bfloat16).reshape(1, token_count, inner_width)
    upstream = upstream_grad.astype(jnp.float32).reshape(block_count, BLOCK, head_count, head_size)
    grad_mixture = (
        upstream - normed * jnp.mean(upstream * normed, axis=-1, keepdims=True)
    ) / row_scale[..., None]
    in_adjoint = jnp.einsum(
        "khq,kqhp,kqn->khpn", enter_weight, grad_mixture, queries, precision=highest
    )
    out_adjoint = jnp.einsum(
        "khq,kqhp,kqn->khpn", leave_weight, grad_mixture, queries, precision=highest
    )
    _, in_total = block_chain(totals, in_adjoint, True, zero_state)
    _, out_total = block_chain(totals, out_adjoint, False, zero_state)
    later_adjoint = entering_2(
        (device_log, in_total), "seq", combine_states, (none_log, zero_state), True
    )[1]
    earlier_adjoint = entering_2(
        (device_log, out_total), "seq", combine_states, (none_log, zero_state), False
    )[1]
    grad_ends, _ = block_chain(totals, in_adjoint, True, later_adjoint)
    grad_starts, _ = block_chain(totals, out_adjoint, False, earlier_adjoint)

    def block_backward(packed):
        (
            block_vals,
            block_keys,
            block_queries,
            block_khalf,
            block_qhalf,
            block_cumul,
            block_logs,
            block_enter,
            block_leave,
            block_end,
            block_start,
            state_in,
            state_next,
            block_grad,
            block_grad_end,
            block_grad_start,
        ) = packed
        affinity = lax.dot_general(
            block_qhalf, block_khalf, (((1,), (1,)), ((), ())), preferred_element_type=jnp.float32
        )

        def group_backward(section):
            group_values, group_cumul, group_logs, group_grad = section
            decays = decay_matrix(group_cumul, group_logs)
            weighted = affinity[None] * decays
            grad_vals = jnp.einsum("gij,igp->jgp", weighted, group_grad, precision=highest)
            grad_weighted = jnp.einsum("igp,jgp->gij", group_grad, group_values, precision=highest)
            return (grad_vals, jnp.sum(grad_weighted * decays, axis=0))

        group_vals, group_affinity = lax.map(
            group_backward,
            (
                to_groups(block_vals, 1, per_group),
                to_groups(block_cumul, 0, per_group),
                to_groups(block_logs, 0, per_group),
                to_groups(block_grad, 1, per_group),
            ),
        )
        grad_affinity = jnp.sum(group_affinity, axis=0)
        enter_cols = block_enter.T[:, :, None]
        leave_cols = block_leave.T[:, :, None]
        end_cols = block_end.T[:, :, None]
        start_cols = block_start.T[:, :, None]
        grad_queries = jnp.dot(grad_affinity, block_keys, precision=highest)
        grad_queries = grad_queries + jnp.einsum(
            "qhp,hpn->qn", block_grad * enter_cols, state_in, precision=highest
        )
        grad_queries = grad_queries + jnp.einsum(
            "qhp,hpn->qn", block_grad * leave_cols, state_next, precision=highest
        )
        grad_keys = jnp.dot(grad_affinity.T, block_queries, precision=highest)
        grad_keys = grad_keys + jnp.einsum(
            "qhp,hpn->qn", block_vals * end_cols, block_grad_end, precision=highest
        )
        grad_keys = grad_keys + jnp.einsum(
            "qhp,hpn->qn", block_vals * start_cols, block_grad_start, precision=highest
        )
        grad_values = from_groups(group_vals, 1)
        grad_values = grad_values + end_cols * jnp.einsum(
            "qn,hpn->qhp", block_keys, block_grad_end, precision=highest
        )
        grad_values = grad_values + start_cols * jnp.einsum(
            "qn,hpn->qhp", block_keys, block_grad_start, precision=highest
        )
        return (grad_values, grad_keys, grad_queries)

    grad_values, grad_keys, grad_queries = lax.map(
        block_backward,
        (
            values,
            key_rows,
            queries,
            key_half,
            query_half,
            cumulative,
            blocked,
            enter_weight,
            leave_weight,
            to_end,
            from_start,
            fwd_in,
            rev_next,
            grad_mixture,
            grad_ends,
            grad_starts,
        ),
    )
    grad_proj = jnp.concatenate(
        [
            grad_values.reshape(token_count, inner_width),
            grad_keys.reshape(token_count, state_size),
            grad_queries.reshape(token_count, state_size),
        ],
        axis=1,
    ).astype(jnp.bfloat16)
    grad_local = lax.dot_general(
        grad_proj,
        lax.all_gather(w_in, "fsdp", axis=0, tiled=True),
        (((1,), (1,)), ((), ())),
        preferred_element_type=jnp.float32,
    )
    grad_tokens = grad_local.astype(jnp.bfloat16).reshape(1, token_count, hidden_width)
    grad_weights = lax.psum_scatter(
        lax.dot_general(
            local_tokens, grad_proj, (((0,), (0,)), ((), ())), preferred_element_type=jnp.float32
        ),
        ("seq", "fsdp"),
        scatter_dimension=0,
        tiled=True,
    )
    return (mixer_out, grad_tokens, grad_weights)


def solution(mesh):
    return jax.shard_map(
        on_device,
        mesh=mesh,
        in_specs=(
            P("fsdp", "seq", None),
            P("fsdp", None),
            P("fsdp", None, "seq"),
            P("fsdp", "seq", None),
        ),
        out_specs=(P("fsdp", "seq", None), P("fsdp", "seq", None), P(("seq", "fsdp"), None)),
        check_vma=False,
    )
```

profile of v0, /device:TPU:0, one launch (start us, length us, event | category | flops | bytes accessed | tf_op | source)
XLA Modules:
  0.0 1677.7 jit_solution(10138005019356209090)
XLA Ops:
  9.2 71.4 %all-gather.11.cloned.1.call-done = bf16[2048,2304]{1,0:T(8,128)(2,1)} async-done(((bf16[512,2304]{1,0:T(8,128)(2,1)}), bf16[2048,2304]{1,0:T(8,128)(2,1)}) %all-gather.11.cloned.1.call-update) | async-done | bytes 9437200 | tf_op jit(solution)/shard_map/all_gather | solution.py:90
  80.6 6.3 convolution_convert_fusion
  87.9 1.6 slice_convert_fusion
  89.5 1.9 copy.58
  91.4 2.8 fusion.93
  96.7 2.8 fusion.96
  100.5 1.6 exponential_bitcast_fusion.4
  103.1 81.3 %all-gather = bf16[32,32,1]{1,2,0:T(2,128)(2,1)S(1)} all-gather(bf16[1,32,1]{1,2,0:T(2,128)(2,1)S(1)} %slice.83), channel_id=2, replica_groups=mesh['seq'=32,'fsdp'=4] {'seq'}, dimensions={0}, use_global_device_ids=true | all-gather | bytes 2112 | tf_op jit(solution)/shard_map/all_gather | solution.py:16
  184.4 2.6 copy.70
  187.0 1.8 fusion.140
  188.8 1.6 broadcast.75.clone
  190.4 18.2 %while.56 = (s32[]{:T(128)}, f32[4,256,8,64]{1,3,2,0:T(8,128)}, f32[4,256,8,64]{1,3,2,0:T(8,128)S(1)}, f32[256,256]{1,0:T(8,128)}, f32[4,8,256]{2,1,0:T(8,128)S(1)}, /*index=5*/f32[4,8,256]{2,1,0:T(8,128)S(1)}, s32[]{:T(128)}) while((s32[]{:T(128)}, f32[4,256,8,64]{1,3,2,0:T(8,128)}, f32[4,256,8,64]{1,3,2,0:T(8,128)S(1)}, ...), condition=%wide.region_3.4_spmd, body=%wide.region_2.3_spmd.sunk | while | flops 406063104 | bytes 2171997 | solution.py:150
  190.4 4.5 fusion.177
  195.0 4.5 fusion.177
  199.6 4.5 fusion.177
  204.1 4.5 fusion.177
  208.6 76.7 %all-gather.15.cloned.1.call-done = bf16[1024,64,128]{2,1,0:T(8,128)(2,1)} async-done(((bf16[32,64,128]{2,1,0:T(8,128)(2,1)}), bf16[1024,64,128]{2,1,0:T(8,128)(2,1)}) %all-gather.15.cloned.1.call-update) | async-done | bytes 16777232 | tf_op jit(solution)/shard_map/all_gather | solution.py:16
  285.4 41.9 %while.58 = (s32[]{:T(128)}, f32[32,64,128]{2,1,0:T(8,128)S(1)}, s32[]{:T(128)}, bf16[32,32]{1,0:T(8,128)(2,1)S(1)}, bf16[32,32,64,128]{3,2,1,0:T(8,128)(2,1)}, ...) while((s32[]{:T(128)}, f32[32,64,128]{2,1,0:T(8,128)S(1)}, s32[]{:T(128)}, bf16[32,32]{1,0:T(8,128)(2,1)S(1)}, ...), condition=%wide.region_7.8_spmd, body=%wide.region_6.7_spmd.sunk | while | flops 786470 | bytes 2621915 | solution.py:31
  327.3 149.6 %all-gather.13.cloned.1.call-done = bf16[1024,64,128]{2,1,0:T(8,128)(2,1)} async-done(((bf16[32,64,128]{2,1,0:T(8,128)(2,1)}), bf16[1024,64,128]{2,1,0:T(8,128)(2,1)}) %all-gather.13.cloned.1.call-update) | async-done | bytes 16777232 | tf_op jit(solution)/shard_map/all_gather | solution.py:16
  477.5 2.0 fusion.133
  479.5 2.3 multiply_reduce_fusion.2
  482.4 1.7 subtract_divide_fusion
  485.5 2.8 fusion.90
  488.3 3.5 fusion.87
  492.1 1.6 broadcast.75
  493.6 35.1 %while.59 = (s32[]{:T(128)}, f32[4,256,8,64]{1,3,2,0:T(8,128)}, f32[4,256,256]{2,1,0:T(8,128)}, f32[4,256,8,64]{1,3,2,0:T(8,128)}, f32[256,256]{1,0:T(8,128)}, /...) while((s32[]{:T(128)}, f32[4,256,8,64]{1,3,2,0:T(8,128)}, ...), condition=%wide.region_12.13_spmd, body=%wide.region_10.12_spmd.sunk | while | flops 812320768 | bytes 5482637 | solution.py:239
  493.7 4.0 multiply_reduce_fusion.4
  498.4 4.0 fusion.183
  502.5 4.0 multiply_reduce_fusion.4
  507.2 4.0 fusion.183
  511.3 4.0 multiply_reduce_fusion.4
  516.0 4.0 fusion.183
  520.1 4.0 multiply_reduce_fusion.4
  524.8 4.0 fusion.183
  530.1 3.7 fusion.105
  533.8 2.0 fusion.108
  535.8 1.8 fusion.114
  537.6 183.1 %all-gather.17.cloned.1.call-done = bf16[1024,64,128]{2,1,0:T(8,128)(2,1)} async-done(((bf16[32,64,128]{2,1,0:T(8,128)(2,1)}), bf16[1024,64,128]{2,1,0:T(8,128)(2,1)}) %all-gather.17.cloned.1.call-update) | async-done | bytes 16777232 | tf_op jit(solution)/shard_map/all_gather | solution.py:16
  720.8 42.2 %while.60 = (s32[]{:T(128)}, f32[32,64,128]{2,1,0:T(8,128)S(1)}, s32[]{:T(128)}, bf16[32,32]{1,0:T(8,128)(2,1)S(1)}, bf16[32,32,64,128]{3,2,1,0:T(8,128)(2,1)}, ...) while((s32[]{:T(128)}, f32[32,64,128]{2,1,0:T(8,128)S(1)}, s32[]{:T(128)}, ...), condition=%wide.region_14.15_spmd, body=%wide.region_13.14_spmd.sunk | while | flops 786470 | bytes 2621915 | solution.py:31
  763.0 4.3 fusion.99
  767.2 3.2 fusion.126
  770.4 140.8 %all-gather.19.cloned.1.call-done = bf16[1024,64,128]{2,1,0:T(8,128)(2,1)} async-done(((bf16[32,64,128]{2,1,0:T(8,128)(2,1)}), bf16[1024,64,128]{2,1,0:T(8,128)(2,1)}) %all-gather.19.cloned.1.call-update) | async-done | bytes 16777232 | tf_op jit(solution)/shard_map/all_gather | solution.py:16
  911.4 3.7 fusion.102
  915.2 2.8 fusion.57
  919.1 8.7 convolution_bitcast_fusion
  927.9 18.7 %copy.74 = f32[2048,2304]{1,0:T(8,128)} copy(f32[2048,2304]{0,1:T(8,128)} %convolution_bitcast_fusion) | data formatting | bytes 37748736
  949.2 7.3 fusion.55
  956.5 714.1 %reduce-scatter.4.cloned.1.call-done = f32[16,2304]{1,0:T(8,128)} async-done(((f32[2048,2304]{1,0:T(8,128)}), f32[16,2304]{1,0:T(8,128)}) %reduce-scatter.4.cloned.1.call-update) | async-done | bytes 147472
  (245 shorter events, 101.0 us)
Async XLA Ops:
  7.2 73.4 %copy-start = (bf16[1,256,2048]{2,1,0:T(8,128)(2,1)S(1)}, bf16[1,256,2048]{2,1,0:T(8,128)(2,1)}, u32[]{:S(2)}) copy-start(bf16[1,256,2048]{2,1,0:T(8,128)(2,1)} %param.16) | copy-start | bytes 3145732
  7.2 0.8 copy-start.9
  7.2 73.4 %all-gather.11.cloned.1.call-start = ((), (), s32[]{:S(2)}) async-start(), calls=%async_computation.1 | async-start | bytes 11796480 | tf_op jit(solution)/shard_map/all_gather | solution.py:90
  7.9 277.4 %all-gather.15.cloned.1.call-start = ((), (), s32[]{:S(2)}) async-start(), calls=%async_computation.3 | async-start | bytes 17301504 | tf_op jit(solution)/shard_map/all_gather | solution.py:16
  9.1 77.8 %copy-start.11 = (f32[1,32,256]{1,2,0:T(8,128)}, f32[1,32,256]{1,2,0:T(8,128)S(1)}, u32[]{:S(2)}) copy-start(f32[1,32,256]{1,2,0:T(8,128)S(1)} %get-tuple-element.649) | copy-start | bytes 98308
  86.9 1.0 copy-start.8
  94.2 382.7 %all-gather.13.cloned.1.call-start = ((), (), s32[]{:S(2)}) async-start(), calls=%async_computation.2 | async-start | bytes 17301504 | tf_op jit(solution)/shard_map/all_gather | solution.py:16
  99.5 621.2 %all-gather.17.cloned.1.call-start = ((), (), s32[]{:S(2)}) async-start(), calls=%async_computation.4 | async-start | bytes 17301504 | tf_op jit(solution)/shard_map/all_gather | solution.py:16
  208.6 76.7 %copy-start.1 = (f32[4,256,8,64]{1,3,2,0:T(8,128)}, f32[4,256,8,64]{1,3,2,0:T(8,128)S(1)}, u32[]{:S(2)}) copy-start(f32[4,256,8,64]{1,3,2,0:T(8,128)S(1)} %get-tuple-element.1040) | copy-start | bytes 6291460
  477.5 2.0 copy-start.6
  479.5 2.3 copy-start.4
  484.1 1.4 copy-start.2
  488.3 423.0 %all-gather.19.cloned.1.call-start = ((), (), s32[]{:S(2)}) async-start(), calls=%async_computation.5 | async-start | bytes 17301504 | tf_op jit(solution)/shard_map/all_gather | solution.py:16
  491.8 1178.8 %reduce-scatter.4.cloned.1.call-start = ((), (), s32[]{:S(2)}) async-start(), calls=%async_computation.6 | async-start | bytes 19021824
  493.7 4.7 copy-start.14
  502.5 4.7 copy-start.14
  511.3 4.7 copy-start.14
  520.0 4.7 copy-start.14
  530.1 3.7 copy-start.3
  911.4 3.7 copy-start.5
  915.2 2.8 copy-start.10
  915.2 3.9 copy-start.12
  946.5 1.2 copy-start.7
  946.6 2.6 copy-start.13
Sparse Core Ops, SparseCore 0:
  9.7 70.8 all-gather.10
  94.3 190.9 all-gather.14
  287.5 189.3 all-gather.12
  488.4 232.2 all-gather.16
  722.2 189.0 all-gather.18
  946.7 723.8 reduce-scatter.3
where the time goes:
time: 1690 us; the launch traced here: 1680 us
  waiting for transfers between devices  1340 us (79%)
  matrix products  112 us (7%)
  other arithmetic  89.8 us (5%)
  blocking collectives  81.3 us (5%)
  local copies, waits for them, and re-layouts  39.6 us (2%)
    unnamed x7, waiting for transfers between devices  715 us
    all_gather x4, waiting for transfers between devices, entering_2(): lax.all_gather(a.astype(kind), axis)  550 us
    all_gather x1, blocking collectives, entering_2(): lax.all_gather(a.astype(kind), axis)  81.3 us
    add x62, other arithmetic, combine_states(): jnp.exp(latter[0])[:, None, None] * earlier[1] + latter[1]  80.9 us
    all_gather x1, waiting for transfers between devices, on_device(): lax.all_gather(w_in, 'fsdp', axis=0, tiled=True)  71.4 us
  transfers between devices with their start and end apart: 6, of which 6 were waited for; matrix products, arithmetic and copies ran while one was open for 11% of the time, Pallas kernels for 0%

commit v1 on v0

--- a/solution.py
+++ b/solution.py
@@ -87,7 +87,9 @@
     per_group = 8
     projected = jnp.dot(
         local_tokens,
-        lax.all_gather(w_in, "fsdp", axis=0, tiled=True),
+        jnp.concatenate(
+            lax.all_to_all(jnp.stack([w_in] * lax.axis_size("fsdp")), "fsdp", 0, 0), axis=0
+        ),
         preferred_element_type=jnp.float32,
     )
     xbc_rows = projected.astype(jnp.bfloat16)

time: 1690 us -> 1750 us (1.036)
  waiting for transfers between devices: 1340 us -> 1370 us
    all_to_all x0 -> x1, waiting for transfers between devices: none -> 105 us  [on_device(): lax.all_to_all(jnp.stack([w_in] * lax.axis_size('fsdp')), 'fsdp', 0, 0)]
    all_gather x1, waiting for transfers between devices: 71.4 us -> 0.01 us  [on_device(): lax.all_gather(w_in, 'fsdp', axis=0, tiled=True)]
    unnamed x7, waiting for transfers between devices: 715 us -> 670 us
    all_gather x4, waiting for transfers between devices: 550 us -> 593 us  [entering_2(): lax.all_gather(a.astype(kind), axis)]
  transfers between devices with their start and end apart: 6 -> 7, of which waited for: 6 -> 6; matrix products, arithmetic and copies ran while one was open for 11% -> 12% of each run, Pallas kernels for 0% -> 0%
where the time goes in v1:
time: 1750 us; the launch traced here: 1730 us
  waiting for transfers between devices  1370 us (78%)
  matrix products  111 us (6%)
  other arithmetic  90.3 us (5%)
  blocking collectives  82.9 us (5%)
  local copies, waits for them, and re-layouts  45.6 us (3%)
    unnamed x7, waiting for transfers between devices  670 us
    all_gather x4, waiting for transfers between devices, entering_2(): lax.all_gather(a.astype(kind), axis)  593 us
    all_to_all x1, waiting for transfers between devices, on_device(): lax.all_to_all(jnp.stack([w_in] * lax.axis_size('fsdp')), 'fsdp', 0, 0)  105 us
    all_gather x1, blocking collectives, entering_2(): lax.all_gather(a.astype(kind), axis)  82.9 us
    add x62, other arithmetic, combine_states(): jnp.exp(latter[0])[:, None, None] * earlier[1] + latter[1]  81.4 us
  transfers between devices with their start and end apart: 7, of which 6 were waited for; matrix products, arithmetic and copies ran while one was open for 12% of the time, Pallas kernels for 0%

profile of v1, /device:TPU:0, one launch (start us, length us, event | category | flops | bytes accessed | tf_op | source)
XLA Modules:
  0.0 1733.6 jit_solution(6493375144948769500)
XLA Ops:
  7.2 6.0 stack.2
  13.2 6.0 all-to-all-start
  20.4 104.9 %all-to-all-done = bf16[4,512,2304]{2,1,0:T(8,128)(2,1)} async-done(((bf16[4,512,2304]{2,1,0:T(8,128)(2,1)}), bf16[4,512,2304]{2,1,0:T(8,128)(2,1)}, u32[]{:S(2)}, u32[]{:S(2)}) %all-to-all-start) | async-done | bytes 9437216 | tf_op jit(solution)/shard_map/all_to_all | solution.py:91
  125.3 6.3 convolution_convert_fusion
  134.2 1.9 copy.58
  136.1 2.8 fusion.93
  141.4 2.8 fusion.96
  145.0 2.6 copy.70
  147.7 1.6 exponential_bitcast_fusion.4
  150.3 82.9 %all-gather = bf16[32,32,1]{1,2,0:T(2,128)(2,1)S(1)} all-gather(bf16[1,32,1]{1,2,0:T(2,128)(2,1)S(1)} %slice.83), channel_id=2, replica_groups=mesh['seq'=32,'fsdp'=4] {'seq'}, dimensions={0}, use_global_device_ids=true | all-gather | bytes 2112 | tf_op jit(solution)/shard_map/all_gather | solution.py:16
  233.3 1.8 fusion.140
  236.6 18.4 %while.56 = (s32[]{:T(128)}, f32[4,256,8,64]{1,3,2,0:T(8,128)}, f32[4,256,8,64]{1,3,2,0:T(8,128)S(1)}, f32[256,256]{1,0:T(8,128)}, f32[4,8,256]{2,1,0:T(8,128)S(1)}, /*index=5*/f32[4,8,256]{2,1,0:T(8,128)S(1)}, s32[]{:T(128)}) while((s32[]{:T(128)}, f32[4,256,8,64]{1,3,2,0:T(8,128)}, f32[4,256,8,64]{1,3,2,0:T(8,128)S(1)}, ...), condition=%wide.region_3.4_spmd, body=%wide.region_2.3_spmd.sunk | while | flops 406063104 | bytes 2171997 | solution.py:152
  236.7 4.5 fusion.177
  241.3 4.5 fusion.177
  245.9 4.5 fusion.177
  250.5 4.5 fusion.177
  255.0 75.7 %all-gather.15.cloned.1.call-done = bf16[1024,64,128]{2,1,0:T(8,128)(2,1)} async-done(((bf16[32,64,128]{2,1,0:T(8,128)(2,1)}), bf16[1024,64,128]{2,1,0:T(8,128)(2,1)}) %all-gather.15.cloned.1.call-update) | async-done | bytes 16777232 | tf_op jit(solution)/shard_map/all_gather | solution.py:16
  330.8 42.0 %while.58 = (s32[]{:T(128)}, f32[32,64,128]{2,1,0:T(8,128)S(1)}, s32[]{:T(128)}, bf16[32,32]{1,0:T(8,128)(2,1)S(1)}, bf16[32,32,64,128]{3,2,1,0:T(8,128)(2,1)}, ...) while((s32[]{:T(128)}, f32[32,64,128]{2,1,0:T(8,128)S(1)}, s32[]{:T(128)}, bf16[32,32]{1,0:T(8,128)(2,1)S(1)}, ...), condition=%wide.region_7.8_spmd, body=%wide.region_6.7_spmd.sunk | while | flops 786470 | bytes 2621915 | solution.py:31
  372.8 148.4 %all-gather.13.cloned.1.call-done = bf16[1024,64,128]{2,1,0:T(8,128)(2,1)} async-done(((bf16[32,64,128]{2,1,0:T(8,128)(2,1)}), bf16[1024,64,128]{2,1,0:T(8,128)(2,1)}) %all-gather.13.cloned.1.call-update) | async-done | bytes 16777232 | tf_op jit(solution)/shard_map/all_gather | solution.py:16
  521.3 12.4 while.57
  533.8 2.0 fusion.133
  535.8 2.3 multiply_reduce_fusion.2
  538.7 1.7 subtract_divide_fusion
  541.8 2.8 fusion.87
  544.6 3.5 fusion.90
  550.3 35.4 %while.59 = (s32[]{:T(128)}, f32[4,256,8,64]{1,3,2,0:T(8,128)}, f32[4,256,256]{2,1,0:T(8,128)}, f32[4,256,8,64]{1,3,2,0:T(8,128)}, f32[256,256]{1,0:T(8,128)}, /...) while((s32[]{:T(128)}, f32[4,256,8,64]{1,3,2,0:T(8,128)}, ...), condition=%wide.region_12.13_spmd, body=%wide.region_10.12_spmd.sunk | while | flops 812320768 | bytes 4434033 | solution.py:241
  550.4 4.1 fusion.183
  554.5 3.9 multiply_reduce_fusion.4
  559.3 4.1 fusion.183
  563.3 3.9 multiply_reduce_fusion.4
  568.1 4.1 fusion.183
  572.2 3.9 multiply_reduce_fusion.4
  576.9 4.1 fusion.183
  581.0 3.9 multiply_reduce_fusion.4
  587.0 3.7 fusion.108
  590.8 2.0 fusion.105
  592.8 1.8 fusion.114
  594.5 183.1 %all-gather.19.cloned.1.call-done = bf16[1024,64,128]{2,1,0:T(8,128)(2,1)} async-done(((bf16[32,64,128]{2,1,0:T(8,128)(2,1)}), bf16[1024,64,128]{2,1,0:T(8,128)(2,1)}) %all-gather.19.cloned.1.call-update) | async-done | bytes 16777232 | tf_op jit(solution)/shard_map/all_gather | solution.py:16
  777.8 4.2 fusion.102
  782.0 185.6 %all-gather.17.cloned.1.call-done = bf16[1024,64,128]{2,1,0:T(8,128)(2,1)} async-done(((bf16[32,64,128]{2,1,0:T(8,128)(2,1)}), bf16[1024,64,128]{2,1,0:T(8,128)(2,1)}) %all-gather.17.cloned.1.call-update) | async-done | bytes 16777232 | tf_op jit(solution)/shard_map/all_gather | solution.py:16
  967.7 42.5 %while.60 = (s32[]{:T(128)}, f32[32,64,128]{2,1,0:T(8,128)S(1)}, s32[]{:T(128)}, bf16[32,32]{1,0:T(8,128)(2,1)S(1)}, bf16[32,32,64,128]{3,2,1,0:T(8,128)(2,1)}, ...) while((s32[]{:T(128)}, f32[32,64,128]{2,1,0:T(8,128)S(1)}, s32[]{:T(128)}, ...), condition=%wide.region_14.15_spmd, body=%wide.region_13.14_spmd.sunk | while | flops 786470 | bytes 2621915 | solution.py:31
  1010.2 3.6 fusion.99
  1015.1 1.9 fusion.126
  1017.0 2.0 fusion.57
  1019.0 8.8 convolution_bitcast_fusion
  1027.8 18.7 %copy.74 = f32[2048,2304]{1,0:T(8,128)} copy(f32[2048,2304]{0,1:T(8,128)} %convolution_bitcast_fusion) | data formatting | bytes 37748736
  1049.1 7.4 fusion.55
  1056.6 669.8 %reduce-scatter.4.cloned.1.call-done = f32[16,2304]{1,0:T(8,128)} async-done(((f32[2048,2304]{1,0:T(8,128)}), f32[16,2304]{1,0:T(8,128)}) %reduce-scatter.4.cloned.1.call-update) | async-done | bytes 147472
  (242 shorter events, 105.5 us)
Async XLA Ops:
  7.2 118.1 %copy-start = (bf16[1,256,2048]{2,1,0:T(8,128)(2,1)S(1)}, bf16[1,256,2048]{2,1,0:T(8,128)(2,1)}, u32[]{:S(2)}) copy-start(bf16[1,256,2048]{2,1,0:T(8,128)(2,1)} %param.16) | copy-start | bytes 3145732
  13.2 6.0 copy-start.9
  13.2 112.1 %all-to-all-start = ((bf16[4,512,2304]{2,1,0:T(8,128)(2,1)}), bf16[4,512,2304]{2,1,0:T(8,128)(2,1)}, u32[]{:S(2)}, u32[]{:S(2)}) async-start(bf16[4,512,2304]{2,1,0:T(8,128)(2,1)} %stack.2), calls=%async_computation | async-start | bytes 18874368 | tf_op jit(solution)/shard_map/all_to_all | solution.py:91
  19.2 311.5 %all-gather.15.cloned.1.call-start = ((), (), s32[]{:S(2)}) async-start(), calls=%async_computation.4 | async-start | bytes 17301504 | tf_op jit(solution)/shard_map/all_gather | solution.py:16
  20.3 111.2 %copy-start.11 = (f32[1,32,256]{1,2,0:T(8,128)}, f32[1,32,256]{1,2,0:T(8,128)S(1)}, u32[]{:S(2)}) copy-start(f32[1,32,256]{1,2,0:T(8,128)S(1)} %get-tuple-element.649) | copy-start | bytes 98308
  131.5 1.1 copy-start.8
  138.9 382.3 %all-gather.13.cloned.1.call-start = ((), (), s32[]{:S(2)}) async-start(), calls=%async_computation.3 | async-start | bytes 17301504 | tf_op jit(solution)/shard_map/all_gather | solution.py:16
  144.2 633.5 %all-gather.19.cloned.1.call-start = ((), (), s32[]{:S(2)}) async-start(), calls=%async_computation.6 | async-start | bytes 17301504 | tf_op jit(solution)/shard_map/all_gather | solution.py:16
  255.0 75.8 %copy-start.1 = (f32[4,256,8,64]{1,3,2,0:T(8,128)}, f32[4,256,8,64]{1,3,2,0:T(8,128)S(1)}, u32[]{:S(2)}) copy-start(f32[4,256,8,64]{1,3,2,0:T(8,128)S(1)} %get-tuple-element.1040) | copy-start | bytes 6291460
  533.8 2.0 copy-start.6
  535.8 2.3 copy-start.4
  540.4 1.4 copy-start.2
  544.5 423.0 %all-gather.17.cloned.1.call-start = ((), (), s32[]{:S(2)}) async-start(), calls=%async_computation.5 | async-start | bytes 17301504 | tf_op jit(solution)/shard_map/all_gather | solution.py:16
  548.1 501.0 %all-gather.11.cloned.1.call-start = ((), (), s32[]{:S(2)}) async-start(), calls=%async_computation.2 | async-start | bytes 11796480 | tf_op jit(solution)/shard_map/all_gather | solution.py:309
  548.7 1177.7 %reduce-scatter.4.cloned.1.call-start = ((), (), s32[]{:S(2)}) async-start(), calls=%async_computation.7 | async-start | bytes 19021824
  587.0 3.7 copy-start.3
  1010.2 3.6 copy-start.10
  1013.9 3.2 copy-start.5
  1015.1 3.9 copy-start.13
  1017.0 2.0 copy-start.12
  1046.5 1.2 copy-start.7
  1046.5 2.6 copy-start.14
Sparse Core Ops, SparseCore 0:
  139.0 191.6 all-gather.14
  332.9 188.2 all-gather.12
  544.7 232.9 all-gather.18
  779.1 188.4 all-gather.16
  969.1 66.9 all-gather.10
  1046.6 679.6 reduce-scatter.3
